TPU v7x, 32 devices: a whole 2x2x4 slice. The times are simulated.
32 devices in a mesh: dp: 2 (over y), expert: 16 (over z, x, core).
Axes of the slice: x: 2, y: 2, z: 4, core: 2. Of those that a mesh axis runs over, the one named last changes fastest.
Arguments:
- tokens: bfloat16 [4096, 2048], P(('dp', 'expert')), may hold values from -6 to 6
- grad_out: bfloat16 [4096, 2048], P(('dp', 'expert')), may hold values from -6 to 6
- expert_ids: int32 [4096, 8], P(('dp', 'expert')), may hold values from 0 to 15, all different within a row; in each aligned block of 128 rows (0 to 127, 128 to 255, ...) at most 72 rows name the same one
- route_weight: bfloat16 [4096, 8], P(('dp', 'expert')), may hold values from 0.049804688 to 1
- w_gate: bfloat16 [16, 2048, 384], P('expert', 'dp'), may hold values from -0.125 to 0.125
- w_up: bfloat16 [16, 2048, 384], P('expert', 'dp'), may hold values from -0.125 to 0.125
- w_down: bfloat16 [16, 384, 2048], P('expert', None, 'dp'), may hold values from -0.3125 to 0.3125
Outputs:
- grad_tokens: bfloat16 [4096, 2048], P(('dp', 'expert'))
- grad_route: bfloat16 [4096, 8], P(('dp', 'expert'))
Inputs may be any that keep to these rules, and one draw needn't show every extreme that they name: `expert_ids`: each row names 8 different experts; among the 128 rows of one device no expert is named by more than 72 rows, and in every draw some expert is named by exactly 72 rows of some device.
All inputs are finite; a program needn't handle non-finite values.
Results may differ from a plain program's by a relative error of at most 0.012.
Values may be sent and summed in bfloat16 or wider, within the bound.
A program may use at most 128 MiB of HBM per device.

v0:
```python
import jax
import jax.numpy as jnp
from jax import lax
from jax.sharding import PartitionSpec as P


def expert_rows(x_rows, g_rows, weight_rows, gate_mat, up_mat, down_mat):
    gate_pre = jnp.dot(x_rows, gate_mat, preferred_element_type=jnp.float32)
    up_pre = jnp.dot(x_rows, up_mat, preferred_element_type=jnp.float32)
    sigmoid_gate = jax.nn.sigmoid(gate_pre)
    active = gate_pre * sigmoid_gate
    hidden = active * up_pre
    back_hidden = jnp.dot(g_rows, down_mat.T, preferred_element_type=jnp.float32)
    route_grad = jnp.sum(hidden * back_hidden, axis=1)
    scaled = weight_rows.astype(jnp.float32)[:, None] * back_hidden
    slope = sigmoid_gate * (1.0 + gate_pre * (1.0 - sigmoid_gate))
    d_gate = (scaled * up_pre * slope).astype(jnp.bfloat16)
    d_up = (scaled * active).astype(jnp.bfloat16)
    input_grad = jnp.dot(d_gate, gate_mat.T, preferred_element_type=jnp.float32) + jnp.dot(
        d_up, up_mat.T, preferred_element_type=jnp.float32
    )
    return (input_grad.astype(jnp.bfloat16), route_grad.astype(jnp.bfloat16))


def per_device(tokens, grad_out, expert_ids, route_weight, w_gate, w_up, w_down):
    tok_rows, width_model = tokens.shape
    n_expert = lax.axis_size("expert")
    gate_mat, up_mat, down_mat = (
        lax.all_gather(w_gate[0], "dp", axis=0, tiled=True),
        lax.all_gather(w_up[0], "dp", axis=0, tiled=True),
        lax.all_gather(w_down[0], "dp", axis=1, tiled=True),
    )
    chosen = expert_ids[:, :, None] == jnp.arange(n_expert, dtype=jnp.int32)[None, None, :]
    dense_w = jnp.sum(
        jnp.where(chosen, route_weight[:, :, None].astype(jnp.float32), 0.0), axis=1
    ).astype(jnp.bfloat16)
    weight_rows = lax.all_to_all(dense_w.T, "expert", split_axis=0, concat_axis=0, tiled=True)
    all_x = lax.all_gather(tokens, "expert", axis=0, tiled=True)
    all_g = lax.all_gather(grad_out, "expert", axis=0, tiled=True)
    out_grad, out_route = expert_rows(
        all_x, all_g, weight_rows.reshape(-1), gate_mat, up_mat, down_mat
    )
    grad_tokens = lax.psum_scatter(out_grad, "expert", scatter_dimension=0, tiled=True)
    back_route = lax.all_to_all(
        out_route.reshape(n_expert, tok_rows), "expert", split_axis=0, concat_axis=0, tiled=True
    )
    grad_route = jnp.sum(
        jnp.where(chosen, back_route.T[:, None, :].astype(jnp.float32), 0.0), axis=2
    ).astype(jnp.bfloat16)
    return (grad_tokens, grad_route)


def solution(mesh):
    return jax.shard_map(
        per_device,
        mesh=mesh,
        in_specs=(
            P(("dp", "expert"), None),
            P(("dp", "expert"), None),
            P(("dp", "expert"), None),
            P(("dp", "expert"), None),
            P("expert", "dp", None),
            P("expert", "dp", None),
            P("expert", None, "dp"),
        ),
        out_specs=(P(("dp", "expert"), None), P(("dp", "expert"), None)),
        check_vma=False,
    )
```

profile of v0, /device:TPU:0, one launch (start us, length us, event | category | flops | bytes accessed | tf_op | source)
XLA Modules:
  0.0 415.4 jit_solution(4736880149228869505)
XLA Ops:
  7.2 0.0 all-gather.17.cloned.1.call-start
  7.2 0.7 all-gather.17.cloned.1.call-update
  7.9 0.0 all-gather.11.cloned.1.call-start
  7.9 0.7 all-gather.11.cloned.1.call-update
  8.6 0.0 all-gather.15.cloned.1.call-start
  8.7 0.7 all-gather.15.cloned.1.call-update
  9.4 0.0 all-gather.13.cloned.1.call-start
  9.4 0.5 all-gather.13.cloned.1.call-update
  10.0 0.0 all-gather.9.cloned.1.call-start
  10.0 0.5 all-gather.9.cloned.1.call-update
  10.5 28.9 %all-gather.17.cloned.1.call-done = bf16[1,2048,384]{2,1,0:T(8,128)(2,1)} async-done(((bf16[1,1024,384]{2,1,0:T(8,128)(2,1)}), bf16[1,2048,384]{2,1,0:T(8,128)(2,1)}) %all-gather.17.cloned.1.call-update) | async-done | bytes 1572880 | tf_op jit(solution)/shard_map/all_gather | solution.py:29
  39.5 76.5 %all-gather.11.cloned.1.call-done = bf16[2048,2048]{1,0:T(8,128)(2,1)} async-done(((bf16[128,2048]{1,0:T(8,128)(2,1)}), bf16[2048,2048]{1,0:T(8,128)(2,1)}) %all-gather.11.cloned.1.call-update) | async-done | bytes 8388624 | tf_op jit(solution)/shard_map/all_gather | solution.py:38
  115.9 6.4 %fusion.3 = f32[2048,384]{0,1:T(8,128)S(1)} fusion(bf16[2048,2048]{1,0:T(8,128)(2,1)} %all-gather.11.cloned.1.call-done, bf16[1,2048,384]{2,1,0:T(8,128)(2,1)} %all-gather.17.cloned.1.call-done), kind=kOutput, calls=%fused_computation.8 | convolution fusion | flops 3221225472 | bytes 13107200 | tf_op jit(solution)/shard_map/dot_general | solution.py:8
  122.3 21.0 %all-gather.15.cloned.1.call-done = bf16[1,2048,384]{2,1,0:T(8,128)(2,1)} async-done(((bf16[1,1024,384]{2,1,0:T(8,128)(2,1)}), bf16[1,2048,384]{2,1,0:T(8,128)(2,1)}) %all-gather.15.cloned.1.call-update) | async-done | bytes 1572880 | tf_op jit(solution)/shard_map/all_gather | solution.py:30
  143.3 8.9 %fusion.6 = f32[2048,384]{0,1:T(8,128)} fusion(bf16[2048,2048]{1,0:T(8,128)(2,1)} %all-gather.11.cloned.1.call-done, bf16[1,2048,384]{2,1,0:T(8,128)(2,1)} %all-gather.15.cloned.1.call-done), kind=kOutput, calls=%fused_computation.11 | convolution fusion | flops 3221225472 | bytes 13107200 | tf_op jit(solution)/shard_map/dot_general | solution.py:9
  152.2 0.0 copy-start.1
  152.2 0.0 copy-start
  152.2 19.7 %all-gather.13.cloned.1.call-done = bf16[1,384,2048]{2,1,0:T(8,128)(2,1)} async-done(((bf16[1,384,1024]{2,1,0:T(8,128)(2,1)}), bf16[1,384,2048]{2,1,0:T(8,128)(2,1)}) %all-gather.13.cloned.1.call-update) | async-done | bytes 1572880 | tf_op jit(solution)/shard_map/all_gather | solution.py:31
  171.9 76.3 %all-gather.9.cloned.1.call-done = bf16[2048,2048]{1,0:T(8,128)(2,1)} async-done(((bf16[128,2048]{1,0:T(8,128)(2,1)}), bf16[2048,2048]{1,0:T(8,128)(2,1)}) %all-gather.9.cloned.1.call-update) | async-done | bytes 8388624 | tf_op jit(solution)/shard_map/all_gather | solution.py:39
  248.2 10.1 %multiply_reduce_fusion = (bf16[2048]{0:T(1024)(128)(2,1)S(1)}, f32[2048,384]{0,1:T(8,128)}) fusion(f32[2048,384]{0,1:T(8,128)} %fusion.6, f32[2048,384]{0,1:T(8,128)S(1)} %fusion.3, bf16[2048,2048]{1,0:T(8,128)(2,1)} %all-gather.9.cloned.1.call-done, bf16[1,384,2048]{2,1,0:T(8,128)(2,1)} %all-gather.13.cloned.1.call-done), kind=kOutput, calls=%fused_computation.1 | convolution fusion | flops 3226728448 | bytes 19402752 | tf_op jit(solution)/shard_map/dot_general | solution.py:13
  258.3 0.6 copy.27
  258.9 3.5 all-to-all-start.1
  262.4 0.0 reduce-scatter.2.cloned.1.call-start
  262.5 0.0 copy-done.1
  262.5 6.3 %all-to-all-done.1 = bf16[16,1,128]{2,1,0:T(2,128)(2,1)S(1)} async-done(((bf16[16,1,128]{2,1,0:T(2,128)(2,1)}), bf16[16,1,128]{2,1,0:T(2,128)(2,1)S(1)}, u32[]{:S(2)}, u32[]{:S(2)}) %all-to-all-start.1) | async-done | bytes 4128 | tf_op jit(solution)/shard_map/all_to_all | solution.py:44
  268.7 0.0 copy-done
  268.8 0.6 select_reduce_fusion
  269.4 9.0 %all_to_all.15 = bf16[16,1,128]{2,1,0:T(2,128)(2,1)S(1)} all-to-all(bf16[16,1,128]{2,1,0:T(2,128)(2,1)S(1)} %copy.25), channel_id=1, replica_groups=mesh['dp'=2,'expert'=16] {'expert'}, dimensions={0} | all-to-all | bytes 8192 | tf_op jit(solution)/shard_map/all_to_all | solution.py:37
  278.4 14.2 %fusion.1 = f32[2048,2048]{1,0:T(8,128)} fusion(f32[2048,384]{0,1:T(8,128)S(1)} %fusion.3, f32[2048,384]{0,1:T(8,128)} %fusion.6, f32[2048,384]{0,1:T(8,128)} %get-tuple-element.5, bf16[1,2048,384]{2,1,0:T(8,128)(2,1)} %all-gather.17.cloned.1.call-done, f32[2048]{0:T(1024)S(1)} %bitcast_convert_fusion), kind=kOutput, calls=%fused_computation.6 | convolution fusion | flops 3229876224 | bytes 27795456 | tf_op jit(solution)/shard_map/dot_general | solution.py:19
  292.6 15.1 %add_convert_fusion = bf16[2048,2048]{1,0:T(8,128)(2,1)} fusion(f32[2048,2048]{1,0:T(8,128)} %fusion.1, f32[2048,384]{0,1:T(8,128)} %get-tuple-element.5, bf16[1,2048,384]{2,1,0:T(8,128)(2,1)} %all-gather.15.cloned.1.call-done, f32[2048]{0:T(1024)S(1)} %bitcast_convert_fusion, f32[2048,384]{0,1:T(8,128)S(1)} %fusion.3), kind=kOutput, calls=%fused_computation | convolution fusion | flops 3235119104 | bytes 33038336 | tf_op jit(solution)/shard_map/dot_general | solution.py:19
  307.7 0.0 reduce-scatter.2.cloned.1.call-update
  307.7 100.8 %reduce-scatter.2.cloned.1.call-done = bf16[128,2048]{1,0:T(8,128)(2,1)} async-done(((bf16[2048,2048]{1,0:T(8,128)(2,1)}), bf16[128,2048]{1,0:T(8,128)(2,1)}) %reduce-scatter.2.cloned.1.call-update) | async-done | bytes 524304 | tf_op jit(solution)/shard_map/reduce_scatter | solution.py:43
  (4 shorter events, 0.0 us)
Async XLA Ops:
  7.2 32.3 %all-gather.17.cloned.1.call-start = ((), (), s32[]{:S(2)}) async-start(), calls=%async_computation.8 | async-start | bytes 2359296 | tf_op jit(solution)/shard_map/all_gather | solution.py:29
  7.9 108.0 %all-gather.11.cloned.1.call-start = ((), (), s32[]{:S(2)}) async-start(), calls=%async_computation.4 | async-start | bytes 8912896 | tf_op jit(solution)/shard_map/all_gather | solution.py:38
  8.6 134.6 %all-gather.15.cloned.1.call-start = ((), (), s32[]{:S(2)}) async-start(), calls=%async_computation.7 | async-start | bytes 2359296 | tf_op jit(solution)/shard_map/all_gather | solution.py:30
  9.4 162.5 %all-gather.13.cloned.1.call-start = ((), (), s32[]{:S(2)}) async-start(), calls=%async_computation.6 | async-start | bytes 2359296 | tf_op jit(solution)/shard_map/all_gather | solution.py:31
  10.0 238.3 %all-gather.9.cloned.1.call-start = ((), (), s32[]{:S(2)}) async-start(), calls=%async_computation.3 | async-start | bytes 8912896 | tf_op jit(solution)/shard_map/all_gather | solution.py:39
  152.2 110.3 %copy-start.1 = (bf16[128,8]{0,1:T(8,128)(2,1)S(1)}, bf16[128,8]{0,1:T(8,128)(2,1)}, u32[]{:S(2)}) copy-start(bf16[128,8]{0,1:T(8,128)(2,1)} %param.10) | copy-start | bytes 6148
  152.2 116.5 %copy-start = (s32[128,8]{0,1:T(8,128)S(1)}, s32[128,8]{0,1:T(8,128)}, u32[]{:S(2)}) copy-start(s32[128,8]{0,1:T(8,128)} %param.9) | copy-start | bytes 12292
  258.9 9.8 %all-to-all-start.1 = ((bf16[16,1,128]{2,1,0:T(2,128)(2,1)}), bf16[16,1,128]{2,1,0:T(2,128)(2,1)S(1)}, u32[]{:S(2)}, u32[]{:S(2)}) async-start(bf16[16,1,128]{2,1,0:T(2,128)(2,1)} %copy.27), calls=%async_computation.2 | async-start | bytes 16384 | tf_op jit(solution)/shard_map/all_to_all | solution.py:44
  262.4 146.1 %reduce-scatter.2.cloned.1.call-start = ((), (), s32[]{:S(2)}) async-start(), calls=%async_computation.5 | async-start | bytes 8912896 | tf_op jit(solution)/shard_map/reduce_scatter | solution.py:43
Sparse Core Ops, SparseCore 0:
  9.5 29.8 all-gather.16
  41.6 74.2 all-gather.10
  117.5 25.7 all-gather.14
  144.7 27.1 all-gather.12
  173.9 74.2 all-gather.8
  307.8 100.6 reduce-scatter.1
where the time goes:
time: 416 us; the launch traced here: 415 us
  waiting for transfers between devices  333 us (80%)
  matrix products  54.6 us (13%)
  between operations  14.2 us (3%)
  blocking collectives  8.99 us (2%)
    reduce_scatter x1, waiting for transfers between devices, per_device(): lax.psum_scatter(out_grad, 'expert', scatter_dimension=0, tiled=True)  101 us
    all_gather x1, waiting for transfers between devices, per_device(): all_x = lax.all_gather(tokens, 'expert', axis=0, tiled=True)  76.5 us
    all_gather x1, waiting for transfers between devices, per_device(): all_g = lax.all_gather(grad_out, 'expert', axis=0, tiled=True)  76.3 us
    all_gather x1, waiting for transfers between devices, per_device(): lax.all_gather(w_gate[0], 'dp', axis=0, tiled=True)  28.9 us
    all_gather x1, waiting for transfers between devices, per_device(): lax.all_gather(w_up[0], 'dp', axis=0, tiled=True)  21 us
    all_gather x1, waiting for transfers between devices, per_device(): lax.all_gather(w_down[0], 'dp', axis=1, tiled=True)  19.7 us
    dot_general x1, matrix products, expert_rows(): jnp.dot(d_up, up_mat.T, preferred_element_type=jnp.float32)  15.1 us
    dot_general x1, matrix products, expert_rows(): jnp.dot(d_gate, gate_mat.T, preferred_element_type=jnp.float32)  14.2 us
  transfers between devices with their start and end apart: 7, of which 7 were waited for; matrix products, arithmetic and copies ran while one was open for 4% of the time, Pallas kernels for 0%

commit v1 on v0

--- a/solution.py
+++ b/solution.py
@@ -35,8 +35,12 @@
         jnp.where(chosen, route_weight[:, :, None].astype(jnp.float32), 0.0), axis=1
     ).astype(jnp.bfloat16)
     weight_rows = lax.all_to_all(dense_w.T, "expert", split_axis=0, concat_axis=0, tiled=True)
-    all_x = lax.all_gather(tokens, "expert", axis=0, tiled=True)
-    all_g = lax.all_gather(grad_out, "expert", axis=0, tiled=True)
+    slabs_push = lambda frame_in, mine, chip_axis: jnp.split(
+        lax.all_gather(jnp.concatenate([frame_in, mine], axis=1), chip_axis, axis=0, tiled=True),
+        [frame_in.shape[1]],
+        axis=1,
+    )
+    all_x, all_g = slabs_push(tokens, grad_out, "expert")
     out_grad, out_route = expert_rows(
         all_x, all_g, weight_rows.reshape(-1), gate_mat, up_mat, down_mat
     )

time: 416 us -> 392 us (0.942)
  waiting for transfers between devices: 333 us -> 305 us
    all_gather x2 -> x1, waiting for transfers between devices: 153 us -> 129 us  [per_device(): lax.all_gather(jnp.concatenate([frame_in, mine], axis=1), chip_axis, axis...]
  transfers between devices with their start and end apart: 7 -> 6, of which waited for: 7 -> 6; matrix products, arithmetic and copies ran while one was open for 4% -> 4% of each run, Pallas kernels for 0% -> 0%
where the time goes in v1:
time: 392 us
  waiting for transfers between devices  305 us (78%)
  matrix products  54.6 us (14%)
  between operations  13.8 us (4%)
  blocking collectives  8.99 us (2%)
  starting transfers between devices  5.82 us (1%)
    all_gather x1, waiting for transfers between devices, per_device(): lax.all_gather(jnp.concatenate([frame_in, mine], axis=1), chip_axis, axis...  129 us
    reduce_scatter x1, waiting for transfers between devices, per_device(): lax.psum_scatter(out_grad, 'expert', scatter_dimension=0, tiled=True)  99.9 us
    all_gather x1, waiting for transfers between devices, per_device(): lax.all_gather(w_gate[0], 'dp', axis=0, tiled=True)  27.9 us
    all_gather x1, waiting for transfers between devices, per_device(): lax.all_gather(w_up[0], 'dp', axis=0, tiled=True)  20.6 us
    all_gather x1, waiting for transfers between devices, per_device(): lax.all_gather(w_down[0], 'dp', axis=1, tiled=True)  19.7 us
    dot_general x1, matrix products, expert_rows(): jnp.dot(d_up, up_mat.T, preferred_element_type=jnp.float32)  15.1 us
    dot_general x1, matrix products, expert_rows(): jnp.dot(d_gate, gate_mat.T, preferred_element_type=jnp.float32)  14.2 us
    dot_general x1, matrix products, expert_rows(): jnp.dot(g_rows, down_mat.T, preferred_element_type=jnp.float32)  10.1 us
  transfers between devices with their start and end apart: 6, of which 6 were waited for; matrix products, arithmetic and copies ran while one was open for 4% of the time, Pallas kernels for 0%

profile of v1, /device:TPU:0, one launch (start us, length us, event | category | flops | bytes accessed | tf_op | source)
XLA Modules:
  0.0 391.7 jit_solution(16998676901793406140)
XLA Ops:
  7.2 0.0 all-gather.14.cloned.1.call-start
  7.2 0.7 all-gather.14.cloned.1.call-update
  7.9 0.0 all-gather.8.cloned.1.call-start
  7.9 2.3 pad_maximum_fusion
  10.2 0.0 all-gather.8.cloned.1.call-update
  10.2 0.0 all-gather.12.cloned.1.call-start
  10.3 0.7 all-gather.12.cloned.1.call-update
  11.0 0.0 all-gather.10.cloned.1.call-start
  11.0 0.5 all-gather.10.cloned.1.call-update
  11.6 27.9 %all-gather.14.cloned.1.call-done = bf16[1,2048,384]{2,1,0:T(8,128)(2,1)} async-done(((bf16[1,1024,384]{2,1,0:T(8,128)(2,1)}), bf16[1,2048,384]{2,1,0:T(8,128)(2,1)}) %all-gather.14.cloned.1.call-update) | async-done | bytes 1572880 | tf_op jit(solution)/shard_map/all_gather | solution.py:29
  39.5 128.6 %all-gather.8.cloned.1.call-done = bf16[2048,4096]{1,0:T(8,128)(2,1)} async-done(((bf16[128,4096]{1,0:T(8,128)(2,1)}), bf16[2048,4096]{1,0:T(8,128)(2,1)}) %all-gather.8.cloned.1.call-update) | async-done | bytes 16777232 | tf_op jit(solution)/shard_map/all_gather | solution.py:39
  168.1 6.4 %fusion.2 = f32[2048,384]{0,1:T(8,128)S(1)} fusion(bf16[2048,4096]{1,0:T(8,128)(2,1)} %all-gather.8.cloned.1.call-done, bf16[1,2048,384]{2,1,0:T(8,128)(2,1)} %all-gather.14.cloned.1.call-done), kind=kOutput, calls=%fused_computation.3 | convolution fusion | flops 3221225472 | bytes 13107200 | tf_op jit(solution)/shard_map/dot_general | solution.py:8
  174.4 20.6 %all-gather.12.cloned.1.call-done = bf16[1,2048,384]{2,1,0:T(8,128)(2,1)} async-done(((bf16[1,1024,384]{2,1,0:T(8,128)(2,1)}), bf16[1,2048,384]{2,1,0:T(8,128)(2,1)}) %all-gather.12.cloned.1.call-update) | async-done | bytes 1572880 | tf_op jit(solution)/shard_map/all_gather | solution.py:30
  195.0 8.9 %fusion.4 = f32[2048,384]{0,1:T(8,128)} fusion(bf16[2048,4096]{1,0:T(8,128)(2,1)} %all-gather.8.cloned.1.call-done, bf16[1,2048,384]{2,1,0:T(8,128)(2,1)} %all-gather.12.cloned.1.call-done), kind=kOutput, calls=%fused_computation.5 | convolution fusion | flops 3221225472 | bytes 13107200 | tf_op jit(solution)/shard_map/dot_general | solution.py:9
  203.9 0.0 copy-start.1
  203.9 0.0 copy-start
  203.9 19.7 %all-gather.10.cloned.1.call-done = bf16[1,384,2048]{2,1,0:T(8,128)(2,1)} async-done(((bf16[1,384,1024]{2,1,0:T(8,128)(2,1)}), bf16[1,384,2048]{2,1,0:T(8,128)(2,1)}) %all-gather.10.cloned.1.call-update) | async-done | bytes 1572880 | tf_op jit(solution)/shard_map/all_gather | solution.py:31
  223.6 10.1 %multiply_reduce_fusion = (bf16[2048]{0:T(1024)(128)(2,1)S(1)}, f32[2048,384]{0,1:T(8,128)}) fusion(f32[2048,384]{0,1:T(8,128)} %fusion.4, f32[2048,384]{0,1:T(8,128)S(1)} %fusion.2, bf16[1,384,2048]{2,1,0:T(8,128)(2,1)} %all-gather.10.cloned.1.call-done, bf16[2048,4096]{1,0:T(8,128)(2,1)} %all-gather.8.cloned.1.call-done), kind=kOutput, calls=%fused_computation.7 | convolution fusion | flops 3226728448 | bytes 19402752 | tf_op jit(solution)/shard_map/dot_general | solution.py:13
  233.7 0.6 copy.27
  234.3 5.6 %all-to-all-start.1 = ((bf16[16,1,128]{2,1,0:T(2,128)(2,1)}), bf16[16,1,128]{2,1,0:T(2,128)(2,1)S(1)}, u32[]{:S(2)}, u32[]{:S(2)}) async-start(bf16[16,1,128]{2,1,0:T(2,128)(2,1)} %copy.27), calls=%async_computation.2 | async-start | bytes 16384 | tf_op jit(solution)/shard_map/all_to_all | solution.py:48
  240.0 0.0 reduce-scatter.2.cloned.1.call-start
  240.0 0.0 copy-done.1
  240.0 6.3 %all-to-all-done.1 = bf16[16,1,128]{2,1,0:T(2,128)(2,1)S(1)} async-done(((bf16[16,1,128]{2,1,0:T(2,128)(2,1)}), bf16[16,1,128]{2,1,0:T(2,128)(2,1)S(1)}, u32[]{:S(2)}, u32[]{:S(2)}) %all-to-all-start.1) | async-done | bytes 4128 | tf_op jit(solution)/shard_map/all_to_all | solution.py:48
  246.3 0.0 copy-done
  246.3 0.6 select_reduce_fusion
  247.0 9.0 %all_to_all.15 = bf16[16,1,128]{2,1,0:T(2,128)(2,1)S(1)} all-to-all(bf16[16,1,128]{2,1,0:T(2,128)(2,1)S(1)} %copy.25), channel_id=1, replica_groups=mesh['dp'=2,'expert'=16] {'expert'}, dimensions={0} | all-to-all | bytes 8192 | tf_op jit(solution)/shard_map/all_to_all | solution.py:37
  256.0 14.2 %fusion.7 = f32[2048,2048]{1,0:T(8,128)} fusion(f32[2048,384]{0,1:T(8,128)S(1)} %fusion.2, f32[2048,384]{0,1:T(8,128)} %fusion.4, f32[2048,384]{0,1:T(8,128)} %get-tuple-element.5, bf16[1,2048,384]{2,1,0:T(8,128)(2,1)} %all-gather.14.cloned.1.call-done, f32[2048]{0:T(1024)S(1)} %bitcast_convert_fusion), kind=kOutput, calls=%fused_computation.12 | convolution fusion | flops 3229876224 | bytes 27795456 | tf_op jit(solution)/shard_map/dot_general | solution.py:19
  270.2 15.1 %add_convert_fusion = bf16[2048,2048]{1,0:T(8,128)(2,1)} fusion(f32[2048,2048]{1,0:T(8,128)} %fusion.7, f32[2048,384]{0,1:T(8,128)} %get-tuple-element.5, bf16[1,2048,384]{2,1,0:T(8,128)(2,1)} %all-gather.12.cloned.1.call-done, f32[2048]{0:T(1024)S(1)} %bitcast_convert_fusion, f32[2048,384]{0,1:T(8,128)S(1)} %fusion.2), kind=kOutput, calls=%fused_computation | convolution fusion | flops 3235119104 | bytes 33038336 | tf_op jit(solution)/shard_map/dot_general | solution.py:19
  285.3 0.0 reduce-scatter.2.cloned.1.call-update
  285.3 99.9 %reduce-scatter.2.cloned.1.call-done = bf16[128,2048]{1,0:T(8,128)(2,1)} async-done(((bf16[2048,2048]{1,0:T(8,128)(2,1)}), bf16[128,2048]{1,0:T(8,128)(2,1)}) %reduce-scatter.2.cloned.1.call-update) | async-done | bytes 524304 | tf_op jit(solution)/shard_map/reduce_scatter | solution.py:47
  (4 shorter events, 0.0 us)
Async XLA Ops:
  7.2 32.3 %all-gather.14.cloned.1.call-start = ((), (), s32[]{:S(2)}) async-start(), calls=%async_computation.7 | async-start | bytes 2359296 | tf_op jit(solution)/shard_map/all_gather | solution.py:29
  7.9 160.2 %all-gather.8.cloned.1.call-start = ((), (), s32[]{:S(2)}) async-start(), calls=%async_computation.3 | async-start | bytes 17825792 | tf_op jit(solution)/shard_map/all_gather | solution.py:39
  10.2 184.8 %all-gather.12.cloned.1.call-start = ((), (), s32[]{:S(2)}) async-start(), calls=%async_computation.6 | async-start | bytes 2359296 | tf_op jit(solution)/shard_map/all_gather | solution.py:30
  11.0 212.7 %all-gather.10.cloned.1.call-start = ((), (), s32[]{:S(2)}) async-start(), calls=%async_computation.5 | async-start | bytes 2359296 | tf_op jit(solution)/shard_map/all_gather | solution.py:31
  203.9 36.1 %copy-start.1 = (bf16[128,8]{0,1:T(8,128)(2,1)S(1)}, bf16[128,8]{0,1:T(8,128)(2,1)}, u32[]{:S(2)}) copy-start(bf16[128,8]{0,1:T(8,128)(2,1)} %param.10) | copy-start | bytes 6148
  203.9 42.4 %copy-start = (s32[128,8]{0,1:T(8,128)S(1)}, s32[128,8]{0,1:T(8,128)}, u32[]{:S(2)}) copy-start(s32[128,8]{0,1:T(8,128)} %param.9) | copy-start | bytes 12292
  234.3 12.0 %all-to-all-start.1 = ((bf16[16,1,128]{2,1,0:T(2,128)(2,1)}), bf16[16,1,128]{2,1,0:T(2,128)(2,1)S(1)}, u32[]{:S(2)}, u32[]{:S(2)}) async-start(bf16[16,1,128]{2,1,0:T(2,128)(2,1)} %copy.27), calls=%async_computation.2 | async-start | bytes 16384 | tf_op jit(solution)/shard_map/all_to_all | solution.py:48
  240.0 145.2 %reduce-scatter.2.cloned.1.call-start = ((), (), s32[]{:S(2)}) async-start(), calls=%async_computation.4 | async-start | bytes 8912896 | tf_op jit(solution)/shard_map/reduce_scatter | solution.py:47
Sparse Core Ops, SparseCore 0:
  9.5 29.9 all-gather.13
  41.6 126.4 all-gather.7
  169.6 25.3 all-gather.11
  196.4 27.1 all-gather.9
  285.4 99.7 reduce-scatter.1
